TPU v7x, 32 devices: a whole 2x2x4 slice. The times are simulated.
32 devices in a mesh: gx: 8 (over y, x, core), gy: 4 (over z).
Axes of the slice: x: 2, y: 2, z: 4, core: 2. Of those that a mesh axis runs over, the one named last changes fastest.
Arguments:
- velocity: float32 [3, 256, 256, 256], P(None, 'gx', 'gy'), may hold values from -4 to 4
- fluid_noise: float32 [3, 256, 256, 256], P(None, 'gx', 'gy'), may hold values from -3 to 3
- cell: int32 [3, 4096], P(None, ('gx', 'gy')), may hold values from 0 to 255, as said below
- offset: float32 [3, 4096], P(None, ('gx', 'gy')), may hold values from 0 to 1
- colloid_velocity: float32 [3, 4096], P(None, ('gx', 'gy')), may hold values from -5 to 5
- particle_noise: float32 [3, 4096], P(None, ('gx', 'gy')), may hold values from -5 to 5
- counts: int32 [32], P(('gx', 'gy')), may hold values from 32 to 128, as said below
Outputs:
- new_velocity: float32 [3, 256, 256, 256], P(None, 'gx', 'gy')
- colloid_force: float32 [3, 4096], P(None, ('gx', 'gy'))
- colloid_drift: float32 [3, 4096], P(None, ('gx', 'gy'))
Inputs may be any that keep to these rules, and one draw needn't show every extreme that they name: `cell`: rows b * 128 to (b + 1) * 128 - 1 form block b. Their first coordinate lies from (b // 4) * 32 up to 32 more, their second from (b mod (4)) * 64 up to 64 more. `counts`: rows of a block at or beyond its count are padding. One block is full in every draw.
All inputs are finite; a program needn't handle non-finite values.
Results may differ from a plain program's by a relative error of at most 0.0003.
Values sent between devices are 32-bit elements; how exact they have to be, the bound alone decides.
No kernel may reach another device: no remote copies, remote signals or barrier semaphores. Data moves between devices by JAX's collectives and lax.ppermute only.
A program may use at most 192 MiB of HBM per device.

v0:
```python
import math
import jax
import jax.numpy as jnp
from jax import lax
from jax.sharding import PartitionSpec as P

drag_rate = 1.0
time_step = 0.5
viscosity = 2.0
exact_products = lax.Precision.HIGHEST


def padded(cells, sides, width):
    for axis, dim in sides:
        count = lax.axis_size(axis)
        head = lax.slice_in_dim(cells, 0, width, axis=dim)
        tail = lax.slice_in_dim(cells, cells.shape[dim] - width, cells.shape[dim], axis=dim)
        cells = jnp.concatenate(
            [
                lax.ppermute(tail, axis, [(i, (i + 1) % count) for i in range(count)]),
                cells,
                lax.ppermute(head, axis, [((i + 1) % count, i) for i in range(count)]),
            ],
            axis=dim,
        )
    return cells


def peskin(gap):
    distance = jnp.abs(gap)
    inner_dist = jnp.minimum(distance, 1.0)
    outer_dist = jnp.clip(distance, 1.0, 2.0)
    near_part = (
        3.0 - 2.0 * inner_dist + jnp.sqrt(1.0 + 4.0 * inner_dist - 4.0 * inner_dist * inner_dist)
    ) / 8.0
    far_part = (
        5.0 - 2.0 * outer_dist - jnp.sqrt(-7.0 + 12.0 * outer_dist - 4.0 * outer_dist * outer_dist)
    ) / 8.0
    return jnp.where(distance < 1.0, near_part, far_part)


def kernel_rows(coords, first_node, node_count, shift, grid_cells):
    nodes = (first_node + jnp.arange(node_count, dtype=jnp.int32)).astype(jnp.float32) + shift
    gap = (
        jnp.mod(coords[:, None] - nodes[None, :] + 0.5 * grid_cells, grid_cells) - 0.5 * grid_cells
    )
    return peskin(gap)


def staggers(component):
    return [0.5 if axis_id == component else 0.0 for axis_id in range(3)]


def widen(field):
    return padded(field, (("gx", 1), ("gy", 2)), 2)


def interpolate(widened, places, x_first, y_first, grid_cells):
    sampled = []
    for component in range(3):
        shifts = staggers(component)
        weight_x = kernel_rows(places[0], x_first - 2, widened.shape[1], shifts[0], grid_cells)
        weight_y = kernel_rows(places[1], y_first - 2, widened.shape[2], shifts[1], grid_cells)
        weight_z = kernel_rows(places[2], 0, widened.shape[3], shifts[2], grid_cells)
        along_z = jnp.einsum("xyz,pz->pxy", widened[component], weight_z, precision=exact_products)
        along_y = jnp.einsum("pxy,py->px", along_z, weight_y, precision=exact_products)
        sampled.append(jnp.sum(along_y * weight_x, axis=1))
    return jnp.stack(sampled)


def twiddle(freq, length):
    columns = jnp.arange(length, dtype=jnp.int32)
    product = freq[:, None] * columns[None, :] % length
    angle = product.astype(jnp.float32) * (2.0 * math.pi / length)
    return (jnp.cos(angle), jnp.sin(angle))


def rotate(spectrum, table, form):
    return jnp.einsum(form, table, spectrum, precision=exact_products)


def block_table(cosine, sine, direction):
    return jnp.stack(
        [jnp.stack([cosine, direction * sine]), jnp.stack([-direction * sine, cosine])]
    )


def project_block(spectrum, freq_x, freq_y, freq_z, grid_cells):
    scale_angle = 2.0 * math.pi / grid_cells
    cos_x = jnp.cos(freq_x.astype(jnp.float32) * scale_angle)[:, None, None]
    sin_x = jnp.sin(freq_x.astype(jnp.float32) * scale_angle)[:, None, None]
    cos_y = jnp.cos(freq_y.astype(jnp.float32) * scale_angle)[None, :, None]
    sin_y = jnp.sin(freq_y.astype(jnp.float32) * scale_angle)[None, :, None]
    cos_z = jnp.cos(freq_z.astype(jnp.float32) * scale_angle)[None, None, :]
    sin_z = jnp.sin(freq_z.astype(jnp.float32) * scale_angle)[None, None, :]
    cos_list = [cos_x, cos_y, cos_z]
    sin_list = [sin_x, sin_y, sin_z]
    anchor = (
        (freq_x[:, None, None] == 0) & (freq_y[None, :, None] == 0) & (freq_z[None, None, :] == 0)
    ).astype(jnp.float32)
    laplace = 2.0 - 2.0 * cos_x + (2.0 - 2.0 * cos_y) + (2.0 - 2.0 * cos_z)
    inverse_lap = 1.0 / (laplace + anchor)
    damping = 1.0 / (1.0 + time_step * viscosity * laplace)
    real_in = spectrum[0]
    imag_in = spectrum[1]
    div_real = 0.0
    div_imag = 0.0
    for axis_id in range(3):
        div_real = (
            div_real
            + (1.0 - cos_list[axis_id]) * real_in[axis_id]
            - sin_list[axis_id] * imag_in[axis_id]
        )
        div_imag = (
            div_imag
            + (1.0 - cos_list[axis_id]) * imag_in[axis_id]
            + sin_list[axis_id] * real_in[axis_id]
        )
    real_out = []
    imag_out = []
    for axis_id in range(3):
        minus_one = cos_list[axis_id] - 1.0
        real_out.append(
            (real_in[axis_id] + (minus_one * div_real - sin_list[axis_id] * div_imag) * inverse_lap)
            * damping
        )
        imag_out.append(
            (imag_in[axis_id] + (minus_one * div_imag + sin_list[axis_id] * div_real) * inverse_lap)
            * damping
        )
    return jnp.stack([jnp.stack(real_out), jnp.stack(imag_out)])


def per_device(velocity, fluid_noise, cell, offset, colloid_velocity, particle_noise, counts):
    slab_cells = velocity.shape[1]
    pencil_cells = velocity.shape[2]
    grid_cells = velocity.shape[3]
    block_rows = cell.shape[1]
    x_first = lax.axis_index("gx") * slab_cells
    y_first = lax.axis_index("gy") * pencil_cells
    places = cell.astype(jnp.float32) + offset
    live = (jnp.arange(block_rows, dtype=jnp.int32) < counts[0]).astype(jnp.float32)
    sampled = interpolate(widen(velocity), places, x_first, y_first, grid_cells)
    colloid_force = live * (drag_rate * (colloid_velocity - sampled) + particle_noise)
    packed = jnp.concatenate([places, colloid_force], axis=0)
    nearby = padded(packed, (("gy", 1),), block_rows)
    spots = nearby[:3]
    loads = nearby[3:]
    layers = []
    for component in range(3):
        shifts = staggers(component)
        weight_x = kernel_rows(spots[0], x_first - 2, slab_cells + 4, shifts[0], grid_cells)
        weight_y = kernel_rows(spots[1], y_first, pencil_cells, shifts[1], grid_cells)
        weight_z = kernel_rows(spots[2], 0, grid_cells, shifts[2], grid_cells)
        plane = (weight_x[:, :, None] * weight_y[:, None, :]).reshape(
            spots.shape[1], (slab_cells + 4) * pencil_cells
        )
        loaded = weight_z * loads[component][:, None]
        layer = jnp.einsum("pa,pz->az", plane, loaded, precision=exact_products)
        layers.append(layer.reshape(slab_cells + 4, pencil_cells, grid_cells))
    spread_field = jnp.stack(layers)
    edge_layers = jnp.concatenate([spread_field[:, :2], spread_field[:, -2:]], axis=1)
    neighbours = padded(edge_layers, (("gx", 1),), 2)
    own_force = spread_field[:, 2:-2]
    own_force = own_force.at[:, :2].add(neighbours[:, :2])
    own_force = own_force.at[:, -2:].add(neighbours[:, -2:])
    rhs = velocity + time_step * own_force + fluid_noise
    freq_kept = jnp.arange(grid_cells, dtype=jnp.int32)
    keep_mask = jnp.ones((grid_cells,), jnp.float32)
    back_weight = jnp.ones((grid_cells,), jnp.float32)
    cos_depth, sin_depth = twiddle(freq_kept, grid_cells)
    forward_table = jnp.stack([cos_depth * keep_mask[:, None], -sin_depth * keep_mask[:, None]])
    spectrum = jnp.einsum("okz,cxyz->ocxyk", forward_table, rhs, precision=exact_products)
    freq_line = jnp.arange(grid_cells, dtype=jnp.int32)
    cos_line, sin_line = twiddle(freq_line, grid_cells)
    forward_block = block_table(cos_line, sin_line, 1.0)
    backward_block = block_table(cos_line, sin_line, -1.0)
    spectrum = lax.all_to_all(spectrum, "gy", split_axis=4, concat_axis=3, tiled=True)
    spectrum = rotate(spectrum, forward_block, "oiky,icxyz->ocxkz")
    spectrum = lax.all_to_all(spectrum, "gx", split_axis=3, concat_axis=2, tiled=True)
    spectrum = rotate(spectrum, forward_block, "oikx,icxyz->ockyz")
    local_y = spectrum.shape[3]
    local_z = spectrum.shape[4]
    freq_y = lax.axis_index("gx") * local_y + jnp.arange(local_y, dtype=jnp.int32)
    freq_z = lax.axis_index("gy") * local_z + jnp.arange(local_z, dtype=jnp.int32)
    spectrum = project_block(spectrum, freq_line, freq_y, freq_z, grid_cells)
    spectrum = rotate(spectrum, backward_block, "oikx,icxyz->ockyz")
    spectrum = lax.all_to_all(spectrum, "gx", split_axis=2, concat_axis=3, tiled=True)
    spectrum = rotate(spectrum, backward_block, "oiky,icxyz->ocxkz")
    spectrum = lax.all_to_all(spectrum, "gy", split_axis=3, concat_axis=4, tiled=True)
    norm_factor = 1.0 / float(grid_cells * grid_cells * grid_cells)
    scaled_weight = (back_weight * norm_factor)[:, None]
    back_table = jnp.stack([cos_depth * scaled_weight, -sin_depth * scaled_weight])
    new_velocity = jnp.einsum("ikz,icxyk->cxyz", back_table, spectrum, precision=exact_products)
    colloid_drift = live * interpolate(widen(new_velocity), places, x_first, y_first, grid_cells)
    return (new_velocity, colloid_force, colloid_drift)


def solution(mesh):
    placed = (
        P(None, "gx", "gy", None),
        P(None, "gx", "gy", None),
        P(None, ("gx", "gy")),
        P(None, ("gx", "gy")),
        P(None, ("gx", "gy")),
        P(None, ("gx", "gy")),
        P(("gx", "gy")),
    )
    return jax.shard_map(
        per_device,
        mesh=mesh,
        in_specs=placed,
        out_specs=(P(None, "gx", "gy", None), P(None, ("gx", "gy")), P(None, ("gx", "gy"))),
        check_vma=False,
    )
```

profile of v0, /device:TPU:0, one launch (start us, length us, event | category | flops | bytes accessed | tf_op | source)
XLA Modules:
  0.0 2014.4 jit_solution(7089020718572155720)
XLA Ops:
  88.3 32.0 %copy.82 = f32[2,3,32,64,256]{3,0,2,1,4:T(2,128)} copy(f32[2,3,32,64,256]{4,3,0,2,1:T(8,128)} %fusion.13) | data formatting | bytes 25165824 | tf_op jit(solution)/shard_map/okz,cxyz->ocxyk/transpose | solution.py:173
  120.2 32.4 %reshape.1211 = f32[4,1,786432]{2,1,0:T(1,128)} reshape(f32[256,3,32,2,64]{4,3,2,1,0:T(2,128)} %bitcast.336) | data formatting | bytes 25165824
  161.3 272.1 %all-to-all-done = f32[4,1,786432]{2,1,0:T(1,128)} async-done(((f32[4,1,786432]{2,1,0:T(1,128)}), f32[4,1,786432]{2,1,0:T(1,128)}, u32[]{:S(2)}, u32[]{:S(2)}) %all-to-all-start) | async-done | bytes 12582944 | tf_op jit(solution)/shard_map/all_to_all | solution.py:178
  434.0 39.7 %reduce.28 = f32[4,786432]{1,0:T(4,128)} reduce(f32[4,1,786432]{2,1,0:T(1,128)} %all-to-all-done, f32[]{:T(128)} %broadcast.2479), dimensions={1}, to_apply=%all_to_all.52.reduce_sub_computation | reduce | bytes 25165828 | tf_op jit(solution)/shard_map/all_to_all | solution.py:178
  473.7 56.0 %reshape.1212 = f32[256,3,32,2,64]{4,3,2,1,0:T(2,128)} reshape(f32[4,786432]{1,0:T(4,128)} %reduce.28) | data formatting | bytes 25165824
  529.7 30.2 %copy.172 = f32[2,3,32,64,4,64]{3,4,5,0,2,1:T(4,128)} copy(f32[2,3,32,64,4,64]{3,0,2,1,5,4:T(2,128)} %bitcast.337) | data formatting | bytes 25165824 | tf_op jit(solution)/shard_map/all_to_all | solution.py:178
  607.9 32.0 %copy.84 = f32[2,3,32,256,64]{4,0,2,1,3:T(2,128)} copy(f32[2,3,32,256,64]{3,4,0,2,1:T(8,128)} %fusion.22) | data formatting | bytes 25165824 | tf_op jit(solution)/shard_map/oiky,icxyz->ocxkz/transpose | solution.py:79
  639.8 29.3 %reshape.1213 = f32[8,1,393216]{2,1,0:T(1,128)} reshape(f32[256,3,32,2,64]{4,3,2,1,0:T(2,128)} %bitcast.339) | data formatting | bytes 25165824
  675.0 138.5 %all-to-all-done.1 = f32[8,1,393216]{2,1,0:T(1,128)} async-done(((f32[8,1,393216]{2,1,0:T(1,128)}), f32[8,1,393216]{2,1,0:T(1,128)}, u32[]{:S(2)}, u32[]{:S(2)}) %all-to-all-start.1) | async-done | bytes 12582944 | tf_op jit(solution)/shard_map/all_to_all | solution.py:180
  813.5 37.1 %reduce.29 = f32[8,393216]{1,0:T(8,128)} reduce(f32[8,1,393216]{2,1,0:T(1,128)} %all-to-all-done.1, f32[]{:T(128)} %broadcast.2479), dimensions={1}, to_apply=%all_to_all.56.reduce_sub_computation | reduce | bytes 25165828 | tf_op jit(solution)/shard_map/all_to_all | solution.py:180
  850.6 41.7 %reshape.1214 = f32[256,3,32,2,64]{4,3,2,1,0:T(2,128)} reshape(f32[8,393216]{1,0:T(8,128)} %reduce.29) | data formatting | bytes 25165824
  927.1 113.1 %fusion.16 = f32[2,3,256,32,64]{2,4,0,3,1:T(8,128)} fusion(f32[2,3,256,32,64,1]{4,3,2,1,0,5:T(8,128)S(1)} %bitcast.334, f32[1,2,256,256]{3,2,1,0:T(8,128)S(1)} %get-tuple-element.60, f32[1,2,256,256]{3,2,1,0:T(8,128)S(1)} %get-tuple-element.63), kind=kOutput, calls=%fused_computation.22 | convolution fusion | flops 19327614976 | bytes 26214400 | tf_op jit(solution)/shard_map/oikx,icxyz->ockyz/dot_general | solution.py:79
  1076.2 32.0 %copy.94 = f32[2,3,256,32,64]{4,0,3,1,2:T(2,128)} copy(f32[2,3,256,32,64]{2,4,0,3,1:T(8,128)} %fusion.25) | data formatting | bytes 25165824 | tf_op jit(solution)/shard_map/oikx,icxyz->ockyz/transpose | solution.py:79
  1108.2 29.7 %reshape.1215 = f32[8,1,393216]{2,1,0:T(1,128)} reshape(f32[256,3,32,2,64]{4,3,2,1,0:T(2,128)} %bitcast.342) | data formatting | bytes 25165824
  1137.9 145.6 %all_to_all.72 = f32[8,1,393216]{2,1,0:T(1,128)} all-to-all(f32[8,1,393216]{2,1,0:T(1,128)} %reshape.1215), channel_id=1, replica_groups=mesh['gx'=8,'gy'=4] {'gx'}, dimensions={0} | all-to-all | bytes 25165824 | tf_op jit(solution)/shard_map/all_to_all | solution.py:188
  1283.6 36.7 %reduce.30 = f32[8,393216]{1,0:T(8,128)} reduce(f32[8,1,393216]{2,1,0:T(1,128)} %all_to_all.72, f32[]{:T(128)} %broadcast.2479), dimensions={1}, to_apply=%all_to_all.60.reduce_sub_computation | reduce | bytes 25165828 | tf_op jit(solution)/shard_map/all_to_all | solution.py:188
  1320.3 41.7 %reshape.1216 = f32[256,3,32,2,64]{4,3,2,1,0:T(2,128)} reshape(f32[8,393216]{1,0:T(8,128)} %reduce.30) | data formatting | bytes 25165824
  1390.8 83.5 %fusion.19 = f32[2,3,32,256,64]{3,4,0,2,1:T(8,128)} fusion(f32[2,3,32,256,64,1]{4,3,2,1,0,5:T(8,128)S(1)} %bitcast.335, f32[1,2,256,256]{3,2,1,0:T(8,128)S(1)} %copy-done.3, f32[1,2,256,256]{3,2,1,0:T(8,128)S(1)} %copy-done.2), kind=kOutput, calls=%fused_computation.23 | convolution fusion | flops 19327614976 | bytes 26214400 | tf_op jit(solution)/shard_map/oiky,icxyz->ocxkz/dot_general | solution.py:79
  1474.4 32.0 %copy.98 = f32[2,3,32,256,64]{4,0,2,1,3:T(2,128)} copy(f32[2,3,32,256,64]{3,4,0,2,1:T(8,128)} %fusion.19) | data formatting | bytes 25165824 | tf_op jit(solution)/shard_map/oiky,icxyz->ocxkz/transpose | solution.py:79
  1506.3 32.4 %reshape.1217 = f32[4,1,786432]{2,1,0:T(1,128)} reshape(f32[256,3,32,2,64]{4,3,2,1,0:T(2,128)} %bitcast.345) | data formatting | bytes 25165824
  1546.1 271.6 %all-to-all-done.3 = f32[4,1,786432]{2,1,0:T(1,128)} async-done(((f32[4,1,786432]{2,1,0:T(1,128)}), f32[4,1,786432]{2,1,0:T(1,128)}, u32[]{:S(2)}, u32[]{:S(2)}) %all-to-all-start.3) | async-done | bytes 12582944 | tf_op jit(solution)/shard_map/all_to_all | solution.py:190
  1817.7 39.9 %reduce.31 = f32[4,786432]{1,0:T(4,128)} reduce(f32[4,1,786432]{2,1,0:T(1,128)} %all-to-all-done.3, f32[]{:T(128)} %broadcast.2479), dimensions={1}, to_apply=%all_to_all.64.reduce_sub_computation | reduce | bytes 25165828 | tf_op jit(solution)/shard_map/all_to_all | solution.py:190
  1857.7 56.0 %reshape.1218 = f32[256,3,32,2,64]{4,3,2,1,0:T(2,128)} reshape(f32[4,786432]{1,0:T(4,128)} %reduce.31) | data formatting | bytes 25165824
  1913.6 30.2 %copy.171 = f32[2,3,32,4,64,64]{5,3,4,0,2,1:T(4,128)} copy(f32[2,3,32,4,64,64]{5,0,2,1,4,3:T(2,128)} %bitcast.346) | data formatting | bytes 25165824 | tf_op jit(solution)/shard_map/all_to_all | solution.py:190
  (161 shorter events, 326.7 us)
Async XLA Ops:
  1.8 10.5 collective-permute-start
  2.4 14.0 collective-permute-start.1
  5.3 51.4 %copy-start.11 = (f32[256]{0:T(256)}, f32[256]{0:T(256)S(1)}, u32[]{:S(2)}) copy-start(f32[256]{0:T(256)S(1)} %iota_convert_fusion) | copy-start | bytes 3076
  5.3 46.3 %copy-start.19 = (f32[256]{0:T(256)}, f32[256]{0:T(256)S(1)}, u32[]{:S(2)}) copy-start(f32[256]{0:T(256)S(1)} %fusion.383) | copy-start | bytes 3076
  5.4 40.5 %copy-start.13 = (f32[36]{0:T(128)}, f32[36]{0:T(128)S(1)}, u32[]{:S(2)}) copy-start(f32[36]{0:T(128)S(1)} %add_convert_fusion) | copy-start | bytes 436
  5.4 40.5 %copy-start.15 = (f32[36]{0:T(128)}, f32[36]{0:T(128)S(1)}, u32[]{:S(2)}) copy-start(f32[36]{0:T(128)S(1)} %broadcast_add_fusion.5) | copy-start | bytes 436
  6.1 34.2 %copy-start.23 = (f32[128]{0:T(128)}, f32[128]{0:T(128)S(1)}, u32[]{:S(2)}) copy-start(f32[128]{0:T(128)S(1)} %compare_convert_fusion) | copy-start | bytes 1540
  6.8 30.7 %copy-start.9 = (f32[128]{0:T(128)}, f32[128]{0:T(128)S(1)}, u32[]{:S(2)}) copy-start(f32[128]{0:T(128)S(1)} %get-tuple-element.71) | copy-start | bytes 1540
  6.8 33.3 %copy-start.17 = (f32[128]{0:T(128)}, f32[128]{0:T(128)S(1)}, u32[]{:S(2)}) copy-start(f32[128]{0:T(128)S(1)} %get-tuple-element.69) | copy-start | bytes 1540
  16.6 12.0 collective-permute-start.2
  19.8 11.2 collective-permute-start.3
  40.4 5.5 collective-permute-start.4
  42.0 3.8 collective-permute-start.5
  62.3 10.5 collective-permute-start.6
  63.4 10.3 collective-permute-start.7
  152.6 280.8 %all-to-all-start = ((f32[4,1,786432]{2,1,0:T(1,128)}), f32[4,1,786432]{2,1,0:T(1,128)}, u32[]{:S(2)}, u32[]{:S(2)}) async-start(f32[4,1,786432]{2,1,0:T(1,128)} %reshape.1211), calls=%async_computation | async-start | bytes 25165824 | tf_op jit(solution)/shard_map/all_to_all | solution.py:178
  669.2 144.3 %all-to-all-start.1 = ((f32[8,1,393216]{2,1,0:T(1,128)}), f32[8,1,393216]{2,1,0:T(1,128)}, u32[]{:S(2)}, u32[]{:S(2)}) async-start(f32[8,1,393216]{2,1,0:T(1,128)} %reshape.1213), calls=%async_computation.1 | async-start | bytes 25165824 | tf_op jit(solution)/shard_map/all_to_all | solution.py:180
  1538.7 279.0 %all-to-all-start.3 = ((f32[4,1,786432]{2,1,0:T(1,128)}), f32[4,1,786432]{2,1,0:T(1,128)}, u32[]{:S(2)}, u32[]{:S(2)}) async-start(f32[4,1,786432]{2,1,0:T(1,128)} %reshape.1217), calls=%async_computation.3 | async-start | bytes 25165824 | tf_op jit(solution)/shard_map/all_to_all | solution.py:190
  1980.2 24.0 %copy-start.1 = (f32[3,32,64,256]{3,2,1,0:T(8,128)}, f32[3,32,64,256]{3,2,1,0:T(8,128)S(1)}, u32[]{:S(2)}) copy-start(f32[3,32,64,256]{3,2,1,0:T(8,128)S(1)} %convolution_bitcast_fusion) | copy-start | bytes 18874372
  1980.3 11.7 collective-permute-start.8
  1980.4 11.6 collective-permute-start.9
  1992.2 10.2 collective-permute-start.10
  1992.3 16.0 copy-start.20
  1992.3 12.0 collective-permute-start.11
  (18 other events, 152.1 us)
where the time goes:
time: 2030 us; the launch traced here: 2010 us
  waiting for transfers between devices  721 us (36%)
  local copies, waits for them, and re-layouts  627 us (31%)
  matrix products  303 us (15%)
  other arithmetic  175 us (9%)
  blocking collectives  146 us (7%)
  starting transfers between devices  40.4 us (2%)
    unnamed x64, local copies, waits for them, and re-layouts  326 us
    all_to_all x1, waiting for transfers between devices, per_device(): lax.all_to_all(spectrum, 'gy', split_axis=4, concat_axis=3, tiled=True)  272 us
    all_to_all x1, waiting for transfers between devices, per_device(): lax.all_to_all(spectrum, 'gy', split_axis=3, concat_axis=4, tiled=True)  272 us
    dot_general x4, matrix products, rotate(): return jnp.einsum(form, table, spectrum, precision=exact_products)  244 us
    all_to_all x1, blocking collectives, per_device(): lax.all_to_all(spectrum, 'gx', split_axis=2, concat_axis=3, tiled=True)  146 us
    all_to_all x1, waiting for transfers between devices, per_device(): lax.all_to_all(spectrum, 'gx', split_axis=3, concat_axis=2, tiled=True)  138 us
    transpose x3, local copies, waits for them, and re-layouts, rotate(): return jnp.einsum(form, table, spectrum, precision=exact_products)  95.9 us
    all_to_all x3, local copies, waits for them, and re-layouts, per_device(): lax.all_to_all(spectrum, 'gy', split_axis=4, concat_axis=3, tiled=True)  54 us
  transfers between devices with their start and end apart: 15, of which 12 were waited for; matrix products, arithmetic and copies ran while one was open for 1% of the time, Pallas kernels for 0%

commit v1 on v0

--- a/solution.py
+++ b/solution.py
@@ -8,6 +8,9 @@
 time_step = 0.5
 viscosity = 2.0
 exact_products = lax.Precision.HIGHEST
+review_trails = lambda sample: jnp.concatenate(
+    jax.lax.all_to_all(jnp.stack(jnp.split(sample, jax.lax.axis_size("gy"), 4), 0), "gy", 0, 0), 3
+)
 
 
 def padded(cells, sides, width):
@@ -175,7 +178,7 @@
     cos_line, sin_line = twiddle(freq_line, grid_cells)
     forward_block = block_table(cos_line, sin_line, 1.0)
     backward_block = block_table(cos_line, sin_line, -1.0)
-    spectrum = lax.all_to_all(spectrum, "gy", split_axis=4, concat_axis=3, tiled=True)
+    spectrum = review_trails(spectrum)
     spectrum = rotate(spectrum, forward_block, "oiky,icxyz->ocxkz")
     spectrum = lax.all_to_all(spectrum, "gx", split_axis=3, concat_axis=2, tiled=True)
     spectrum = rotate(spectrum, forward_block, "oikx,icxyz->ockyz")

time: 2030 us -> 2020 us (level)
  local copies, waits for them, and re-layouts: 627 us -> 604 us
    reshape x0 -> x3, local copies, waits for them, and re-layouts: none -> 69.4 us  [jnp.concatenate(jax.lax.all_to_all(jnp.stack(jnp.split(sample, jax.lax.ax...]
    all_to_all x3 -> x1, local copies, waits for them, and re-layouts: 54 us -> 0.59 us  [jax.lax.all_to_all(jnp.stack(jnp.split(sample, jax.lax.axis_size('gy'), 4...]
    transpose x1 -> x0, local copies, waits for them, and re-layouts: 32 us -> none  [per_device(): jnp.einsum('okz,cxyz->ocxyk', forward_table, rhs, precision=exact_products)]
    unnamed x64, local copies, waits for them, and re-layouts: 326 us -> 304 us
where the time goes in v1:
time: 2020 us; the launch traced here: 2010 us
  waiting for transfers between devices  722 us (36%)
  local copies, waits for them, and re-layouts  604 us (30%)
  matrix products  302 us (15%)
  other arithmetic  191 us (9%)
  blocking collectives  146 us (7%)
  starting transfers between devices  40.4 us (2%)
    unnamed x64, local copies, waits for them, and re-layouts  304 us
    all_to_all x1, waiting for transfers between devices, jax.lax.all_to_all(jnp.stack(jnp.split(sample, jax.lax.axis_size('gy'), 4...  272 us
    all_to_all x1, waiting for transfers between devices, per_device(): lax.all_to_all(spectrum, 'gy', split_axis=3, concat_axis=4, tiled=True)  272 us
    dot_general x4, matrix products, rotate(): return jnp.einsum(form, table, spectrum, precision=exact_products)  244 us
    all_to_all x1, blocking collectives, per_device(): lax.all_to_all(spectrum, 'gx', split_axis=2, concat_axis=3, tiled=True)  146 us
    all_to_all x1, waiting for transfers between devices, per_device(): lax.all_to_all(spectrum, 'gx', split_axis=3, concat_axis=2, tiled=True)  138 us
    transpose x3, local copies, waits for them, and re-layouts, rotate(): return jnp.einsum(form, table, spectrum, precision=exact_products)  95.8 us
    reshape x3, local copies, waits for them, and re-layouts, jnp.concatenate(jax.lax.all_to_all(jnp.stack(jnp.split(sample, jax.lax.ax...  69.4 us
  transfers between devices with their start and end apart: 15, of which 12 were waited for; matrix products, arithmetic and copies ran while one was open for 1% of the time, Pallas kernels for 0%

profile of v1, /device:TPU:0, one launch (start us, length us, event | category | flops | bytes accessed | tf_op | source)
XLA Modules:
  0.0 2007.1 jit_solution(12043265142980597526)
XLA Ops:
  120.4 33.5 %reshape.1220 = f32[4,1,786432]{2,1,0:T(1,128)} reshape(f32[4,3,32,2,64,64]{5,4,3,2,1,0:T(8,128)} %fusion.509) | data formatting | bytes 25165824
  162.5 272.1 %all-to-all-done = f32[4,1,786432]{2,1,0:T(1,128)} async-done(((f32[4,1,786432]{2,1,0:T(1,128)}), f32[4,1,786432]{2,1,0:T(1,128)}, u32[]{:S(2)}, u32[]{:S(2)}) %all-to-all-start) | async-done | bytes 12582944 | tf_op jit(solution)/shard_map/all_to_all | solution.py:12
  435.2 39.6 %reduce.28 = f32[4,786432]{1,0:T(4,128)} reduce(f32[4,1,786432]{2,1,0:T(1,128)} %all-to-all-done, f32[]{:T(128)} %broadcast.2479), dimensions={1}, to_apply=%all_to_all.42.reduce_sub_computation | reduce | bytes 25165828 | tf_op jit(solution)/shard_map/all_to_all | solution.py:12
  474.8 32.1 %reshape.1221 = f32[4,3,32,2,64,64]{5,4,3,2,1,0:T(8,128)} reshape(f32[4,786432]{1,0:T(4,128)} %reduce.28) | data formatting | bytes 25165824
  524.5 28.6 %copy.144 = f32[2,3,32,4,64,64]{4,3,5,0,2,1:T(4,128)} copy(f32[2,3,32,4,64,64]{5,4,0,2,1,3:T(8,128)} %bitcast_bitcast_fusion) | data formatting | bytes 25165824 | tf_op jit(solution)/shard_map/reshape | solution.py:11
  600.6 31.9 %copy.84 = f32[2,3,32,256,64]{4,0,2,1,3:T(2,128)} copy(f32[2,3,32,256,64]{3,4,0,2,1:T(8,128)} %fusion.22) | data formatting | bytes 25165824 | tf_op jit(solution)/shard_map/oiky,icxyz->ocxkz/transpose | solution.py:82
  632.6 29.3 %reshape.1222 = f32[8,1,393216]{2,1,0:T(1,128)} reshape(f32[256,3,32,2,64]{4,3,2,1,0:T(2,128)} %bitcast.344) | data formatting | bytes 25165824
  667.8 138.5 %all-to-all-done.1 = f32[8,1,393216]{2,1,0:T(1,128)} async-done(((f32[8,1,393216]{2,1,0:T(1,128)}), f32[8,1,393216]{2,1,0:T(1,128)}, u32[]{:S(2)}, u32[]{:S(2)}) %all-to-all-start.1) | async-done | bytes 12582944 | tf_op jit(solution)/shard_map/all_to_all | solution.py:183
  806.2 36.9 %reduce.29 = f32[8,393216]{1,0:T(8,128)} reduce(f32[8,1,393216]{2,1,0:T(1,128)} %all-to-all-done.1, f32[]{:T(128)} %broadcast.2479), dimensions={1}, to_apply=%all_to_all.43.reduce_sub_computation | reduce | bytes 25165828 | tf_op jit(solution)/shard_map/all_to_all | solution.py:183
  843.2 41.8 %reshape.1223 = f32[256,3,32,2,64]{4,3,2,1,0:T(2,128)} reshape(f32[8,393216]{1,0:T(8,128)} %reduce.29) | data formatting | bytes 25165824
  885.0 24.9 %copy.85 = f32[2,3,32,256,64]{4,3,2,1,0:T(8,128)} copy(f32[2,3,32,256,64]{4,0,2,1,3:T(2,128)} %bitcast.345) | data formatting | bytes 25165824 | tf_op jit(solution)/shard_map/all_to_all | solution.py:183
  919.7 113.2 %fusion.16 = f32[2,3,256,32,64]{2,4,0,3,1:T(8,128)} fusion(f32[2,3,256,32,64,1]{4,3,2,1,0,5:T(8,128)S(1)} %bitcast.342, f32[1,2,256,256]{3,2,1,0:T(8,128)S(1)} %get-tuple-element.64, f32[1,2,256,256]{3,2,1,0:T(8,128)S(1)} %get-tuple-element.67), kind=kOutput, calls=%fused_computation.26 | convolution fusion | flops 19327614976 | bytes 26214400 | tf_op jit(solution)/shard_map/oikx,icxyz->ockyz/dot_general | solution.py:82
  1069.0 31.9 %copy.94 = f32[2,3,256,32,64]{4,0,3,1,2:T(2,128)} copy(f32[2,3,256,32,64]{2,4,0,3,1:T(8,128)} %fusion.25) | data formatting | bytes 25165824 | tf_op jit(solution)/shard_map/oikx,icxyz->ockyz/transpose | solution.py:82
  1100.9 29.7 %reshape.1224 = f32[8,1,393216]{2,1,0:T(1,128)} reshape(f32[256,3,32,2,64]{4,3,2,1,0:T(2,128)} %bitcast.347) | data formatting | bytes 25165824
  1130.6 145.7 %all_to_all.59 = f32[8,1,393216]{2,1,0:T(1,128)} all-to-all(f32[8,1,393216]{2,1,0:T(1,128)} %reshape.1224), channel_id=1, replica_groups=mesh['gx'=8,'gy'=4] {'gx'}, dimensions={0} | all-to-all | bytes 25165824 | tf_op jit(solution)/shard_map/all_to_all | solution.py:191
  1276.3 36.7 %reduce.30 = f32[8,393216]{1,0:T(8,128)} reduce(f32[8,1,393216]{2,1,0:T(1,128)} %all_to_all.59, f32[]{:T(128)} %broadcast.2479), dimensions={1}, to_apply=%all_to_all.47.reduce_sub_computation | reduce | bytes 25165828 | tf_op jit(solution)/shard_map/all_to_all | solution.py:191
  1313.0 41.7 %reshape.1225 = f32[256,3,32,2,64]{4,3,2,1,0:T(2,128)} reshape(f32[8,393216]{1,0:T(8,128)} %reduce.30) | data formatting | bytes 25165824
  1383.6 83.5 %fusion.19 = f32[2,3,32,256,64]{3,4,0,2,1:T(8,128)} fusion(f32[2,3,32,256,64,1]{4,3,2,1,0,5:T(8,128)S(1)} %bitcast.343, f32[1,2,256,256]{3,2,1,0:T(8,128)S(1)} %copy-done.3, f32[1,2,256,256]{3,2,1,0:T(8,128)S(1)} %copy-done.2), kind=kOutput, calls=%fused_computation.27 | convolution fusion | flops 19327614976 | bytes 26214400 | tf_op jit(solution)/shard_map/oiky,icxyz->ocxkz/dot_general | solution.py:82
  1467.1 32.0 %copy.98 = f32[2,3,32,256,64]{4,0,2,1,3:T(2,128)} copy(f32[2,3,32,256,64]{3,4,0,2,1:T(8,128)} %fusion.19) | data formatting | bytes 25165824 | tf_op jit(solution)/shard_map/oiky,icxyz->ocxkz/transpose | solution.py:82
  1499.0 32.4 %reshape.1226 = f32[4,1,786432]{2,1,0:T(1,128)} reshape(f32[256,3,32,2,64]{4,3,2,1,0:T(2,128)} %bitcast.350) | data formatting | bytes 25165824
  1538.8 271.6 %all-to-all-done.3 = f32[4,1,786432]{2,1,0:T(1,128)} async-done(((f32[4,1,786432]{2,1,0:T(1,128)}), f32[4,1,786432]{2,1,0:T(1,128)}, u32[]{:S(2)}, u32[]{:S(2)}) %all-to-all-start.3) | async-done | bytes 12582944 | tf_op jit(solution)/shard_map/all_to_all | solution.py:193
  1810.4 39.9 %reduce.31 = f32[4,786432]{1,0:T(4,128)} reduce(f32[4,1,786432]{2,1,0:T(1,128)} %all-to-all-done.3, f32[]{:T(128)} %broadcast.2479), dimensions={1}, to_apply=%all_to_all.51.reduce_sub_computation | reduce | bytes 25165828 | tf_op jit(solution)/shard_map/all_to_all | solution.py:193
  1850.3 56.0 %reshape.1227 = f32[256,3,32,2,64]{4,3,2,1,0:T(2,128)} reshape(f32[4,786432]{1,0:T(4,128)} %reduce.31) | data formatting | bytes 25165824
  1906.3 30.2 %copy.172 = f32[2,3,32,4,64,64]{5,3,4,0,2,1:T(4,128)} copy(f32[2,3,32,4,64,64]{5,0,2,1,4,3:T(2,128)} %bitcast.351) | data formatting | bytes 25165824 | tf_op jit(solution)/shard_map/all_to_all | solution.py:193
  (163 shorter events, 351.0 us)
Async XLA Ops:
  1.8 10.5 collective-permute-start
  2.4 14.0 collective-permute-start.1
  5.3 51.4 %copy-start.11 = (f32[256]{0:T(256)}, f32[256]{0:T(256)S(1)}, u32[]{:S(2)}) copy-start(f32[256]{0:T(256)S(1)} %iota_convert_fusion) | copy-start | bytes 3076
  5.3 46.3 %copy-start.19 = (f32[256]{0:T(256)}, f32[256]{0:T(256)S(1)}, u32[]{:S(2)}) copy-start(f32[256]{0:T(256)S(1)} %fusion.383) | copy-start | bytes 3076
  5.4 40.5 %copy-start.13 = (f32[36]{0:T(128)}, f32[36]{0:T(128)S(1)}, u32[]{:S(2)}) copy-start(f32[36]{0:T(128)S(1)} %add_convert_fusion) | copy-start | bytes 436
  5.4 40.5 %copy-start.15 = (f32[36]{0:T(128)}, f32[36]{0:T(128)S(1)}, u32[]{:S(2)}) copy-start(f32[36]{0:T(128)S(1)} %broadcast_add_fusion.5) | copy-start | bytes 436
  6.1 34.2 %copy-start.23 = (f32[128]{0:T(128)}, f32[128]{0:T(128)S(1)}, u32[]{:S(2)}) copy-start(f32[128]{0:T(128)S(1)} %compare_convert_fusion) | copy-start | bytes 1540
  6.8 30.7 %copy-start.9 = (f32[128]{0:T(128)}, f32[128]{0:T(128)S(1)}, u32[]{:S(2)}) copy-start(f32[128]{0:T(128)S(1)} %get-tuple-element.75) | copy-start | bytes 1540
  6.8 33.3 %copy-start.17 = (f32[128]{0:T(128)}, f32[128]{0:T(128)S(1)}, u32[]{:S(2)}) copy-start(f32[128]{0:T(128)S(1)} %get-tuple-element.73) | copy-start | bytes 1540
  16.6 12.0 collective-permute-start.2
  19.8 11.2 collective-permute-start.3
  40.4 5.5 collective-permute-start.4
  42.0 3.8 collective-permute-start.5
  63.0 10.9 collective-permute-start.6
  64.1 10.5 collective-permute-start.7
  153.9 280.8 %all-to-all-start = ((f32[4,1,786432]{2,1,0:T(1,128)}), f32[4,1,786432]{2,1,0:T(1,128)}, u32[]{:S(2)}, u32[]{:S(2)}) async-start(f32[4,1,786432]{2,1,0:T(1,128)} %reshape.1220), calls=%async_computation | async-start | bytes 25165824 | tf_op jit(solution)/shard_map/all_to_all | solution.py:12
  661.9 144.3 %all-to-all-start.1 = ((f32[8,1,393216]{2,1,0:T(1,128)}), f32[8,1,393216]{2,1,0:T(1,128)}, u32[]{:S(2)}, u32[]{:S(2)}) async-start(f32[8,1,393216]{2,1,0:T(1,128)} %reshape.1222), calls=%async_computation.1 | async-start | bytes 25165824 | tf_op jit(solution)/shard_map/all_to_all | solution.py:183
  1531.4 279.0 %all-to-all-start.3 = ((f32[4,1,786432]{2,1,0:T(1,128)}), f32[4,1,786432]{2,1,0:T(1,128)}, u32[]{:S(2)}, u32[]{:S(2)}) async-start(f32[4,1,786432]{2,1,0:T(1,128)} %reshape.1226), calls=%async_computation.3 | async-start | bytes 25165824 | tf_op jit(solution)/shard_map/all_to_all | solution.py:193
  1972.9 24.0 %copy-start.1 = (f32[3,32,64,256]{3,2,1,0:T(8,128)}, f32[3,32,64,256]{3,2,1,0:T(8,128)S(1)}, u32[]{:S(2)}) copy-start(f32[3,32,64,256]{3,2,1,0:T(8,128)S(1)} %convolution_bitcast_fusion) | copy-start | bytes 18874372
  1973.0 11.7 collective-permute-start.8
  1973.1 11.6 collective-permute-start.9
  1984.9 10.2 collective-permute-start.10
  1985.0 16.0 copy-start.20
  1985.0 12.0 collective-permute-start.11
  (18 other events, 152.5 us)
